TPU v7x, 128 devices: a whole 4x4x4 slice. The times are simulated.
128 devices in a mesh: seq: 32 (over x, y, core), head: 4 (over z).
Axes of the slice: x: 4, y: 4, z: 4, core: 2. Of those that a mesh axis runs over, the one named last changes fastest.
Arguments:
- vis_tokens: bfloat16 [12288, 1408], P('seq'), may hold values from -70 to 70
- vis_counts: int32 [4, 8], replicated, may hold values from 1 to 384, 1536 in all within a row
- vis_spatial: int32 [4, 96], replicated, may hold values from 0 to 1023, as said below
- enc_gain: float32 [1408], replicated, may hold values from 0.25 to 1.75
- enc_bias: float32 [1408], replicated, may hold values from -3 to 3
- enc_qkv: bfloat16 [3, 1408, 1408], P(None, None, 'head'), may hold values from -6 to 6
- enc_proj: bfloat16 [1408, 1408], P('head'), may hold values from -0.15625 to 0.15625
- final_gain: float32 [1408], replicated, may hold values from 0.25 to 1.75
- final_bias: float32 [1408], replicated, may hold values from -3 to 3
- to_decoder: bfloat16 [1408, 512], replicated, may hold values from -0.15625 to 0.15625
- mask_token: float32 [512], replicated, may hold values from -4 to 4
- dec_gain: float32 [512], replicated, may hold values from 0.25 to 1.75
- dec_bias: float32 [512], replicated, may hold values from -3 to 3
- dec_qkv: bfloat16 [3, 512, 512], P(None, None, 'head'), may hold values from -11 to 11
Outputs:
- decoded: bfloat16 [4, 16, 1024, 512], P(None, None, 'seq', 'head')
Inputs may be any that keep to these rules, and one draw needn't show every extreme that they name: `vis_spatial`: row c lists in increasing order the spatial positions visible in every frame of clip c; each aligned run of 32 spatial positions holds exactly 3 of them. The visible tokens of clip c, in order of position, lie on the members of its encoder group in order, vis_counts[c, g] of them on member g; each row sums to 1536.
All inputs are finite; a program needn't handle non-finite values.
Results may differ from a plain program's by a relative error of at most 0.015.
Values may be sent and summed in bfloat16 or wider, within the bound.
A program may use at most 320 MiB of HBM per device.

v0:
```python
import math
import jax
import jax.numpy as jnp
from jax import lax
from jax.sharding import PartitionSpec as P

D = 1408
HEADS = 16
DD = 512
DHEADS = 8
S = 1024
BLOCK = 32
GROUP = 8
L = 16384
VSP = 96
VIS = 1536
epsilon = 1e-06
floor_score = -1e30


def from_partner(block, axis, distance):
    count = lax.axis_size(axis)
    route = []
    for low in range(count):
        high = low | 1 << distance
        if high != low and high < count:
            route += [(low, high), (high, low)]
    return lax.ppermute(block, axis, route)


def layer_norm(values, gain_row, bias_row):
    centre = jnp.mean(values, axis=-1, keepdims=True)
    centred = values - centre
    spread = jnp.mean(centred * centred, axis=-1, keepdims=True)
    return centred * lax.rsqrt(spread + epsilon) * gain_row + bias_row


def sinusoid(positions, table_width):
    column_ids = jnp.arange(table_width, dtype=jnp.int32)
    exponent = (2 * (column_ids // 2)).astype(jnp.float32) / table_width
    frequency = jnp.exp(exponent * -math.log(10000.0))
    angles = positions.astype(jnp.float32)[:, None] * frequency[None, :]
    return jnp.where(column_ids[None, :] % 2 == 0, jnp.sin(angles), jnp.cos(angles))


def fold_block(fold_state, queries, key_rows, value_rows, allowed, score_scale):
    running_max, running_sum, running_acc = fold_state
    scores = jnp.einsum("cqhe,ckhe->chqk", queries, key_rows, preferred_element_type=jnp.float32)
    allowed_grid = allowed[:, None, None, :]
    scores = jnp.where(allowed_grid, scores * score_scale, floor_score)
    new_max = jnp.maximum(running_max, jnp.max(scores, axis=-1))
    factor = jnp.exp(running_max - new_max)
    raised = jnp.where(allowed_grid, jnp.exp(scores - new_max[..., None]), 0.0)
    running_sum = running_sum * factor + jnp.sum(raised, axis=-1)
    weights = raised.astype(jnp.bfloat16)
    update = jnp.einsum("chqk,ckhe->chqe", weights, value_rows, preferred_element_type=jnp.float32)
    running_acc = running_acc * factor[..., None] + update
    return (new_max, running_sum, running_acc)


def empty_state(batch_count, head_count, query_count, head_size):
    return (
        jnp.full((batch_count, head_count, query_count), floor_score, jnp.float32),
        jnp.zeros((batch_count, head_count, query_count), jnp.float32),
        jnp.zeros((batch_count, head_count, query_count, head_size), jnp.float32),
    )


def body(
    vis_tokens,
    vis_counts,
    vis_spatial,
    enc_gain,
    enc_bias,
    enc_qkv,
    enc_proj,
    final_gain,
    final_bias,
    to_decoder,
    mask_token,
    dec_gain,
    dec_bias,
    dec_qkv,
):
    seq_count = lax.axis_size("seq")
    seq_index = lax.axis_index("seq")
    clips = vis_counts.shape[0]
    clip_index = seq_index % clips
    member = seq_index // clips
    slot_count = vis_tokens.shape[0]
    slot_ids = jnp.arange(slot_count, dtype=jnp.int32)
    member_ids = jnp.arange(GROUP, dtype=jnp.int32)
    group_counts = lax.dynamic_index_in_dim(vis_counts, clip_index, 0, keepdims=False)
    before = jnp.sum(jnp.where(member_ids < member, group_counts, 0))
    slot_live = slot_ids < jnp.sum(jnp.where(member_ids == member, group_counts, 0))
    token_rows = vis_tokens.astype(jnp.float32)
    normed = layer_norm(token_rows, enc_gain, enc_bias).astype(jnp.bfloat16)
    enc_parts = [
        jnp.dot(normed, enc_qkv[part_id], preferred_element_type=jnp.float32).astype(jnp.bfloat16)
        for part_id in range(3)
    ]
    head_size = D // HEADS
    enc_width = enc_parts[0].shape[1]
    local_heads = enc_width // head_size
    enc_queries = enc_parts[0].reshape(1, slot_count, local_heads, head_size)
    key_value = jnp.stack([enc_parts[1], enc_parts[2]])
    enc_scale = 1.0 / math.sqrt(head_size)
    clip_bits = clips.bit_length() - 1
    collected = key_value[None]
    for bit in range(GROUP.bit_length() - 1):
        partner = from_partner(collected, "seq", bit + clip_bits)
        upper_side = (member >> bit) % 2 == 1
        collected = jnp.where(
            upper_side,
            jnp.concatenate([partner, collected], axis=0),
            jnp.concatenate([collected, partner], axis=0),
        )
    group_keys = jnp.moveaxis(collected, 1, 0).reshape(
        2, 1, GROUP * slot_count, local_heads, head_size
    )
    group_live = (slot_ids[None, :] < group_counts[:, None]).reshape(1, GROUP * slot_count)
    fold_state = fold_block(
        empty_state(1, local_heads, slot_count, head_size),
        enc_queries,
        group_keys[0],
        group_keys[1],
        group_live,
        enc_scale,
    )
    context = fold_state[2][0] / fold_state[1][0][..., None]
    context = jnp.transpose(context, (1, 0, 2)).reshape(slot_count, enc_width).astype(jnp.bfloat16)
    partial_out = jnp.dot(context, enc_proj, preferred_element_type=jnp.float32)
    attended = lax.psum(partial_out.astype(jnp.bfloat16), "head").astype(jnp.float32)
    residual = token_rows + attended
    final_rows = layer_norm(residual, final_gain, final_bias).astype(jnp.bfloat16)
    encoded = jnp.dot(final_rows, to_decoder, preferred_element_type=jnp.float32).astype(
        jnp.bfloat16
    )
    visible_index = jnp.minimum(before + slot_ids, VIS - 1)
    spatial_row = lax.dynamic_index_in_dim(vis_spatial, clip_index, 0, keepdims=False)
    spatial_ids = jnp.arange(VSP, dtype=jnp.int32)
    spatial = jnp.sum(
        jnp.where((visible_index % VSP)[:, None] == spatial_ids[None, :], spatial_row[None, :], 0),
        axis=1,
    )
    position = visible_index // VSP * S + spatial
    block_index = position // BLOCK
    owner_index = block_index % seq_count
    own_rows = L // seq_count
    local_row = clip_index * own_rows + block_index // seq_count * BLOCK + position % BLOCK
    per_peer = slot_count // seq_count
    peer_ids = jnp.arange(seq_count, dtype=jnp.int32)
    owner_hits = ((owner_index[:, None] == peer_ids[None, :]) & slot_live[:, None]).astype(
        jnp.float32
    )
    earlier_mask = (slot_ids[None, :] < slot_ids[:, None]).astype(jnp.float32)
    earlier = jnp.dot(earlier_mask, owner_hits, precision=lax.Precision.HIGHEST)
    bucket_rank = jnp.sum(earlier * owner_hits, axis=1).astype(jnp.int32)
    target = jnp.where(slot_live, owner_index * per_peer + bucket_rank, -1)
    bucket_ids = jnp.arange(seq_count * per_peer, dtype=jnp.int32)
    chosen = target[None, :] == bucket_ids[:, None]
    send_rows = (
        jnp.dot(chosen.astype(jnp.bfloat16), encoded, preferred_element_type=jnp.float32)
        .astype(jnp.bfloat16)
        .reshape(seq_count, per_peer, DD)
    )
    send_index = jnp.max(jnp.where(chosen, local_row[None, :], -1), axis=1).reshape(
        seq_count, per_peer
    )
    got_rows, got_index = (
        lax.all_to_all(send_rows, "seq", split_axis=0, concat_axis=0, tiled=True),
        lax.all_to_all(send_index, "seq", split_axis=0, concat_axis=0, tiled=True),
    )
    total_rows = clips * own_rows
    got_index = jnp.where(got_index < 0, total_rows, got_index).reshape(-1)
    placed = (
        jnp.zeros((total_rows, DD), jnp.float32)
        .at[got_index]
        .set(got_rows.reshape(-1, DD).astype(jnp.float32), mode="drop")
    )
    row_ids = jnp.arange(own_rows, dtype=jnp.int32)
    local_position = (row_ids // BLOCK * seq_count + seq_index) * BLOCK + row_ids % BLOCK
    frame_ids = jnp.arange(S, dtype=jnp.int32)
    spatial_flags = jnp.any(vis_spatial[:, :, None] == frame_ids[None, None, :], axis=1)
    column_pick = ((local_position % S)[:, None] == frame_ids[None, :]).astype(jnp.float32)
    seen_flags = (
        jnp.einsum(
            "cs,rs->cr",
            spatial_flags.astype(jnp.float32),
            column_pick,
            precision=lax.Precision.HIGHEST,
        )
        > 0.5
    )
    inputs = sinusoid(local_position, DD)[None] + jnp.where(
        seen_flags[..., None], placed.reshape(clips, own_rows, DD), mask_token[None, None, :]
    )
    dec_normed = layer_norm(inputs, dec_gain, dec_bias).astype(jnp.bfloat16)
    dec_size = DD // DHEADS
    dec_query = jnp.einsum(
        "crd,de->cre", dec_normed, dec_qkv[0], preferred_element_type=jnp.float32
    ).astype(jnp.bfloat16)
    dec_width = dec_query.shape[2]
    dec_heads = dec_width // dec_size
    dec_queries = dec_query.reshape(clips, own_rows, dec_heads, dec_size)
    dec_scale = 1.0 / math.sqrt(dec_size)
    start_state = empty_state(clips, dec_heads, own_rows, dec_size)
    dec_key = jnp.einsum(
        "crd,de->cre", dec_normed, dec_qkv[1], preferred_element_type=jnp.float32
    ).astype(jnp.bfloat16)
    dec_value = jnp.einsum(
        "crd,de->cre", dec_normed, dec_qkv[2], preferred_element_type=jnp.float32
    ).astype(jnp.bfloat16)
    stacked = jnp.stack([dec_key, dec_value])
    shard_part = lax.all_gather(stacked, "seq", axis=2, tiled=True)
    row_count = shard_part.shape[2]
    block_count = row_count // own_rows
    block_rows = row_count // block_count
    grouped = jnp.moveaxis(
        shard_part.reshape(2, clips, block_count, block_rows, dec_heads, dec_size), 2, 0
    )
    everywhere = jnp.ones((clips, block_rows), dtype=bool)

    def scan_step(inner_state, key_block):
        return (
            fold_block(inner_state, dec_queries, key_block[0], key_block[1], everywhere, dec_scale),
            None,
        )

    result_state, _ = lax.scan(scan_step, start_state, grouped)
    fold_state = result_state
    dec_context = fold_state[2] / fold_state[1][..., None]
    dec_context = jnp.transpose(dec_context, (0, 2, 1, 3)).reshape(
        clips, own_rows // BLOCK, BLOCK, dec_width
    )
    return dec_context.astype(jnp.bfloat16)


def solution(mesh):
    in_specs = (
        P("seq", None),
        P(),
        P(),
        P(),
        P(),
        P(None, None, "head"),
        P("head", None),
        P(),
        P(),
        P(),
        P(),
        P(),
        P(),
        P(None, None, "head"),
    )
    out_specs = P(None, None, "seq", "head")
    return jax.shard_map(body, mesh=mesh, in_specs=in_specs, out_specs=out_specs, check_vma=False)
```

profile of v0, /device:TPU:1, one launch (start us, length us, event | category | flops | bytes accessed | tf_op | source)
XLA Modules:
  0.0 682.2 jit_solution(31880487049167066)
XLA Ops:
  14.1 3.8 collective-permute-start
  17.9 11.9 %collective-permute-done = bf16[1,2,384,352]{2,3,1,0:T(8,128)(2,1)} collective-permute-done((bf16[1,2,384,352]{2,3,1,0:T(8,128)(2,1)S(1)}, bf16[1,2,384,352]{2,3,1,0:T(8,128)(2,1)}, u32[]{:S(2)}, u32[]{:S(2)}) %collective-permute-start) | collective-permute-done | bytes 540704 | tf_op jit(solution)/shard_map/ppermute | solution.py:28
  33.3 23.1 %collective-permute-done.1 = bf16[2,2,384,352]{2,3,1,0:T(8,128)(2,1)} collective-permute-done((bf16[2,2,384,352]{2,3,1,0:T(8,128)(2,1)}, bf16[2,2,384,352]{2,3,1,0:T(8,128)(2,1)}, u32[]{:S(2)}, u32[]{:S(2)}) %collective-permute-start.1) | collective-permute-done | bytes 1081376 | tf_op jit(solution)/shard_map/ppermute | solution.py:28
  56.4 4.0 maximum_select_fusion.1
  68.0 40.4 %collective-permute-done.2 = bf16[4,2,384,352]{2,3,1,0:T(8,128)(2,1)} collective-permute-done((bf16[4,2,384,352]{2,3,1,0:T(8,128)(2,1)}, bf16[4,2,384,352]{2,3,1,0:T(8,128)(2,1)}, u32[]{:S(2)}, u32[]{:S(2)}) %collective-permute-start.2) | collective-permute-done | bytes 2162720 | tf_op jit(solution)/shard_map/ppermute | solution.py:28
  108.5 3.9 fusion.22
  116.3 4.2 reshape.477
  120.5 3.7 copy.37
  124.2 4.7 reshape.478
  128.9 11.2 %fusion.16 = (f32[4,384]{1,0:T(4,128)S(1)}, f32[4,384,3072]{2,1,0:T(8,128)}) fusion(pred[3072]{0:T(1024)(128)(4,1)S(1)} %lt.153, bf16[384,4,88]{0,2,1:T(8,128)(2,1)S(1)} %bitcast.138, bf16[3072,4,88]{0,2,1:T(8,128)(2,1)} %reshape.477), kind=kOutput, calls=%fused_computation.24 | convolution fusion | flops 844626432 | bytes 21316608 | tf_op jit(solution)/shard_map/cqhe,ckhe->chqk/dot_general | solution.py:48
  140.1 11.2 %fusion.17 = f32[4,384]{1,0:T(4,128)S(1)} fusion(f32[4,384,3072]{2,1,0:T(8,128)} %get-tuple-element.105, f32[4,384]{1,0:T(4,128)S(1)} %get-tuple-element.103, pred[3072]{0:T(1024)(128)(4,1)S(1)} %lt.153), kind=kLoop, calls=%fused_computation.25 | loop fusion | flops 23591424 | bytes 18889728 | tf_op jit(solution)/shard_map/reduce_sum | solution.py:54
  151.4 12.2 %fusion.62 = bf16[384,4,88]{0,2,1:T(8,128)(2,1)} fusion(bf16[3072,4,88]{0,2,1:T(8,128)(2,1)} %reshape.478, f32[4,384,3072]{2,1,0:T(8,128)} %get-tuple-element.105, f32[4,384]{1,0:T(4,128)S(1)} %get-tuple-element.103, pred[3072]{0:T(1024)(128)(4,1)S(1)} %lt.153, f32[384,4]{0,1:T(4,128)S(1)} %bitcast_add_fusion.1, f32[384,4]{0,1:T(4,128)S(1)} %get-tuple-element.102), kind=kOutput, calls=%fused_computation.86 | convolution fusion | flops 854470656 | bytes 21328896 | tf_op jit(solution)/shard_map/chqk,ckhe->chqe/dot_general | solution.py:56
  168.7 10.2 %all-to-all-start = ((s32[32,1,12]{2,1,0:T(1,128)}), s32[32,1,12]{2,1,0:T(1,128)S(1)}, u32[]{:S(2)}, u32[]{:S(2)}) async-start(s32[32,1,12]{2,1,0:T(1,128)} %bitcast.3), calls=%async_computation | async-start | bytes 32768 | tf_op jit(solution)/shard_map/all_to_all | solution.py:172
  179.9 36.2 %all-reduce.2.cloned.1.call-done = bf16[384,1408]{1,0:T(8,128)(2,1)} async-done(((bf16[384,1408]{1,0:T(8,128)(2,1)}), bf16[384,1408]{1,0:T(8,128)(2,1)}) %all-reduce.2.cloned.1.call-update) | async-done | bytes 1081360 | tf_op jit(solution)/shard_map/psum | solution.py:133
  221.6 9.3 %all-to-all-start.1 = ((bf16[32,12,512]{2,1,0:T(8,128)(2,1)}), bf16[32,12,512]{2,1,0:T(8,128)(2,1)S(1)}, u32[]{:S(2)}, u32[]{:S(2)}) async-start(bf16[32,12,512]{2,1,0:T(8,128)(2,1)} %reshape.479), calls=%async_computation.1 | async-start | bytes 1048576 | tf_op jit(solution)/shard_map/all_to_all | solution.py:171
  231.0 3.7 fusion.57
  236.2 6.3 all-to-all-done.1
  242.6 4.0 scatter_custom_fusion
  246.6 3.0 fusion.23
  257.6 108.6 %all-gather.2.cloned.1.call-done = bf16[2,4,16384,128]{3,2,1,0:T(8,128)(2,1)} async-done(((bf16[2,4,512,128]{3,2,1,0:T(8,128)(2,1)}), bf16[2,4,16384,128]{3,2,1,0:T(8,128)(2,1)}) %all-gather.2.cloned.1.call-update) | async-done | bytes 33554448 | tf_op jit(solution)/shard_map/all_gather | solution.py:215
  366.1 44.1 %copy.38 = bf16[2,4,16384,128]{2,3,1,0:T(8,128)(2,1)} copy(bf16[2,4,16384,128]{3,2,1,0:T(8,128)(2,1)} %all-gather.2.cloned.1.call-done) | data formatting | bytes 67108864 | tf_op jit(solution)/shard_map/all_gather | solution.py:215
  410.2 22.7 %copy.45 = bf16[128,8,32,512]{3,2,1,0:T(8,128)(2,1)} copy(bf16[128,8,32,512]{3,1,2,0:T(8,128)(2,1)} %bitcast.132) | data formatting | bytes 67108864
  432.9 22.9 %copy.40 = bf16[32,2,4,512,2,64]{3,5,4,2,1,0:T(8,128)(2,1)} copy(bf16[32,2,4,512,2,64]{3,0,5,4,2,1:T(8,128)(2,1)} %bitcast.133) | data formatting | bytes 67108864
  455.8 217.1 %while.15 = (s32[]{:T(128)}, f32[4,2,512]{2,1,0:T(2,128)S(1)}, f32[4,2,512]{2,1,0:T(2,128)S(1)}, f32[4,2,512,64]{2,3,1,0:T(8,128)S(1)}, bf16[32,2,4,512,2,64]{3,...) while((s32[]{:T(128)}, f32[4,2,512]{2,1,0:T(2,128)S(1)}, ...), condition=%wide.region_19.20_spmd.clone, body=%wide.region_16.19_spmd.clone.sunk | while | flops 554455040 | bytes 29098120 | solution.py:230
  (290 shorter events, 261.2 us)
Async XLA Ops:
  6.5 211.8 %copy-start = (bf16[1408,512]{1,0:T(8,128)(2,1)S(1)}, bf16[1408,512]{1,0:T(8,128)(2,1)}, u32[]{:S(2)}) copy-start(bf16[1408,512]{1,0:T(8,128)(2,1)} %param.25) | copy-start | bytes 4325380
  6.5 3.3 copy-start.4
  6.5 3.3 copy-start.12
  6.5 3.3 copy-start.13
  6.5 209.5 %all-reduce.2.cloned.1.call-start = ((), (), s32[]{:S(2)}) async-start(), calls=%async_computation.2 | async-start | bytes 2162688 | tf_op jit(solution)/shard_map/psum | solution.py:133
  14.1 15.7 %collective-permute-start = (bf16[1,2,384,352]{2,3,1,0:T(8,128)(2,1)S(1)}, bf16[1,2,384,352]{2,3,1,0:T(8,128)(2,1)}, u32[]{:S(2)}, u32[]{:S(2)}) collective-permute-start(bf16[1,2,384,352]{2,3,1,0:T(8,128)(2,1)S(1)} %maximum_bitcast_fusion), channel_id=1, source_target_pairs={{0,16},{16,0},{4,20},{20,4},{8,24},{24,8},{12,28},{28,12},{32,48},... | collective-permute-start | bytes 1622024 | tf_op jit(solution)/shard_map/ppermute | solution.py:28
  32.2 24.3 %collective-permute-start.1 = (bf16[2,2,384,352]{2,3,1,0:T(8,128)(2,1)}, bf16[2,2,384,352]{2,3,1,0:T(8,128)(2,1)}, u32[]{:S(2)}, u32[]{:S(2)}) collective-permute-start(bf16[2,2,384,352]{2,3,1,0:T(8,128)(2,1)} %maximum_select_fusion.2), channel_id=1, source_target_pairs={{0,32},{32,0},{4,36},{36,4},{8,40},{40,8},{12,44},{44,12},{16,48},... | collective-permute-start | bytes 3244040 | tf_op jit(solution)/shard_map/ppermute | solution.py:28
  33.3 31.1 %copy-start.11 = (s32[4,96]{1,0:T(4,128)S(1)}, s32[4,96]{1,0:T(4,128)}, u32[]{:S(2)}) copy-start(s32[4,96]{1,0:T(4,128)} %param.18) | copy-start | bytes 4612
  60.4 48.1 %collective-permute-start.2 = (bf16[4,2,384,352]{2,3,1,0:T(8,128)(2,1)}, bf16[4,2,384,352]{2,3,1,0:T(8,128)(2,1)}, u32[]{:S(2)}, u32[]{:S(2)}) collective-permute-start(bf16[4,2,384,352]{2,3,1,0:T(8,128)(2,1)} %maximum_select_fusion.1), channel_id=1, source_target_pairs={{0,64},{64,0},{4,68},{68,4},{8,72},{72,8},{12,76},{76,12},{16,80},... | collective-permute-start | bytes 6488072 | tf_op jit(solution)/shard_map/ppermute | solution.py:28
  151.4 12.2 %copy-start.6 = (bf16[352,1408]{1,0:T(8,128)(2,1)S(1)}, bf16[352,1408]{1,0:T(8,128)(2,1)}, u32[]{:S(2)}) copy-start(bf16[352,1408]{1,0:T(8,128)(2,1)} %param.22) | copy-start | bytes 2973700
  168.7 52.9 %all-to-all-start = ((s32[32,1,12]{2,1,0:T(1,128)}), s32[32,1,12]{2,1,0:T(1,128)S(1)}, u32[]{:S(2)}, u32[]{:S(2)}) async-start(s32[32,1,12]{2,1,0:T(1,128)} %bitcast.3), calls=%async_computation | async-start | bytes 32768 | tf_op jit(solution)/shard_map/all_to_all | solution.py:172
  179.8 38.5 %copy-start.14 = (f32[1408]{0:T(1024)S(1)}, f32[1408]{0:T(1024)}, u32[]{:S(2)}) copy-start(f32[1408]{0:T(1024)} %param.24) | copy-start | bytes 16900
  179.8 38.5 %copy-start.15 = (f32[1408]{0:T(1024)S(1)}, f32[1408]{0:T(1024)}, u32[]{:S(2)}) copy-start(f32[1408]{0:T(1024)} %param.23) | copy-start | bytes 16900
  216.1 1.7 copy-start.5
  221.6 20.9 %all-to-all-start.1 = ((bf16[32,12,512]{2,1,0:T(8,128)(2,1)}), bf16[32,12,512]{2,1,0:T(8,128)(2,1)S(1)}, u32[]{:S(2)}, u32[]{:S(2)}) async-start(bf16[32,12,512]{2,1,0:T(8,128)(2,1)} %reshape.479), calls=%async_computation.1 | async-start | bytes 1048576 | tf_op jit(solution)/shard_map/all_to_all | solution.py:171
  230.9 135.2 %all-gather.2.cloned.1.call-start = ((), (), s32[]{:S(2)}) async-start(), calls=%async_computation.3 | async-start | bytes 34603008 | tf_op jit(solution)/shard_map/all_gather | solution.py:215
  242.6 4.0 copy-start.8
  246.6 3.4 copy-start.2
  250.0 1.3 copy-start.9
  250.0 1.3 copy-start.10
  251.4 1.2 copy-start.7
  252.6 1.4 copy-start.3
  672.9 2.2 copy-start.1
Sparse Core Ops, SparseCore 0:
  166.5 49.5 all-reduce.1
  255.2 110.8 all-gather.1
where the time goes:
time: 693 us; the launch traced here: 682 us
  waiting for transfers between devices  227 us (33%)
  matrix products  207 us (30%)
  local copies, waits for them, and re-layouts  115 us (17%)
  other arithmetic  90.4 us (13%)
  starting transfers between devices  27.2 us (4%)
  between operations  14.1 us (2%)
    all_gather x1, waiting for transfers between devices, body(): shard_part = lax.all_gather(stacked, 'seq', axis=2, tiled=True)  109 us
    dot_general x33, matrix products, fold_block(): jnp.einsum('chqk,ckhe->chqe', weights, value_rows, preferred_element_type...  105 us
    dot_general x33, matrix products, fold_block(): jnp.einsum('cqhe,ckhe->chqk', queries, key_rows, preferred_element_type=j...  86.7 us
    ppermute x3, waiting for transfers between devices, from_partner(): return lax.ppermute(block, axis, route)  75.4 us
    reduce_sum x33, other arithmetic, fold_block(): running_sum = running_sum * factor + jnp.sum(raised, axis=-1)  56.9 us
    unnamed x35, local copies, waits for them, and re-layouts  46.1 us
    all_gather x1, local copies, waits for them, and re-layouts, body(): shard_part = lax.all_gather(stacked, 'seq', axis=2, tiled=True)  44.1 us
    psum x1, waiting for transfers between devices, body(): lax.psum(partial_out.astype(jnp.bfloat16), 'head').astype(jnp.float32)  36.2 us
  transfers between devices with their start and end apart: 7, of which 6 were waited for; matrix products, arithmetic and copies ran while one was open for 3% of the time, Pallas kernels for 0%

commit v1 on v0

--- a/solution.py
+++ b/solution.py
@@ -212,7 +212,9 @@
         "crd,de->cre", dec_normed, dec_qkv[2], preferred_element_type=jnp.float32
     ).astype(jnp.bfloat16)
     stacked = jnp.stack([dec_key, dec_value])
-    shard_part = lax.all_gather(stacked, "seq", axis=2, tiled=True)
+    shard_part = jnp.concatenate(
+        lax.all_to_all(jnp.stack([stacked] * lax.axis_size("seq")), "seq", 0, 0), axis=2
+    )
     row_count = shard_part.shape[2]
     block_count = row_count // own_rows
     block_rows = row_count // block_count

time: 693 us -> 1060 us (1.53)
  the two profiles are of different devices: /device:TPU:1 before, /device:TPU:12 now
where the time goes in v1:
time: 1060 us; the launch traced here: 1050 us
  waiting for transfers between devices  669 us (63%)
  matrix products  207 us (20%)
  other arithmetic  89.4 us (8%)
  local copies, waits for them, and re-layouts  37.1 us (4%)
  starting transfers between devices  27.3 us (3%)
  between operations  14.1 us (1%)
    all_to_all x1, waiting for transfers between devices, body(): lax.all_to_all(jnp.stack([stacked] * lax.axis_size('seq')), 'seq', 0, 0)  547 us
    dot_general x33, matrix products, fold_block(): jnp.einsum('chqk,ckhe->chqe', weights, value_rows, preferred_element_type...  105 us
    dot_general x33, matrix products, fold_block(): jnp.einsum('cqhe,ckhe->chqk', queries, key_rows, preferred_element_type=j...  86.7 us
    ppermute x3, waiting for transfers between devices, from_partner(): return lax.ppermute(block, axis, route)  80.6 us
    reduce_sum x33, other arithmetic, fold_block(): running_sum = running_sum * factor + jnp.sum(raised, axis=-1)  56.9 us
    psum x1, waiting for transfers between devices, body(): lax.psum(partial_out.astype(jnp.bfloat16), 'head').astype(jnp.float32)  38.1 us
  transfers between devices with their start and end apart: 7, of which 6 were waited for; matrix products, arithmetic and copies ran while one was open for 2% of the time, Pallas kernels for 0%

profile of v1, /device:TPU:12, one launch (start us, length us, event | category | flops | bytes accessed | tf_op | source)
XLA Modules:
  0.0 1045.9 jit_solution(2690552517032975872)
XLA Ops:
  16.4 13.3 %collective-permute-done = bf16[1,2,384,352]{2,3,1,0:T(8,128)(2,1)} collective-permute-done((bf16[1,2,384,352]{2,3,1,0:T(8,128)(2,1)S(1)}, bf16[1,2,384,352]{2,3,1,0:T(8,128)(2,1)}, u32[]{:S(2)}, u32[]{:S(2)}) %collective-permute-start) | collective-permute-done | bytes 540704 | tf_op jit(solution)/shard_map/ppermute | solution.py:28
  33.4 23.9 %collective-permute-done.1 = bf16[2,2,384,352]{2,3,1,0:T(8,128)(2,1)} collective-permute-done((bf16[2,2,384,352]{2,3,1,0:T(8,128)(2,1)}, bf16[2,2,384,352]{2,3,1,0:T(8,128)(2,1)}, u32[]{:S(2)}, u32[]{:S(2)}) %collective-permute-start.1) | collective-permute-done | bytes 1081376 | tf_op jit(solution)/shard_map/ppermute | solution.py:28
  57.2 4.0 maximum_select_fusion.1
  66.7 43.4 %collective-permute-done.2 = bf16[4,2,384,352]{2,3,1,0:T(8,128)(2,1)} collective-permute-done((bf16[4,2,384,352]{2,3,1,0:T(8,128)(2,1)}, bf16[4,2,384,352]{2,3,1,0:T(8,128)(2,1)}, u32[]{:S(2)}, u32[]{:S(2)}) %collective-permute-start.2) | collective-permute-done | bytes 2162720 | tf_op jit(solution)/shard_map/ppermute | solution.py:28
  110.1 3.9 fusion.22
  117.9 4.2 reshape.479
  122.2 3.7 copy.35
  125.8 4.7 reshape.480
  130.5 11.2 %fusion.16 = (f32[4,384]{1,0:T(4,128)S(1)}, f32[4,384,3072]{2,1,0:T(8,128)}) fusion(pred[3072]{0:T(1024)(128)(4,1)S(1)} %lt.153, bf16[384,4,88]{0,2,1:T(8,128)(2,1)S(1)} %bitcast.132, bf16[3072,4,88]{0,2,1:T(8,128)(2,1)} %reshape.479), kind=kOutput, calls=%fused_computation.24 | convolution fusion | flops 844626432 | bytes 21316608 | tf_op jit(solution)/shard_map/cqhe,ckhe->chqk/dot_general | solution.py:48
  141.8 11.2 %fusion.17 = f32[4,384]{1,0:T(4,128)S(1)} fusion(f32[4,384,3072]{2,1,0:T(8,128)} %get-tuple-element.87, f32[4,384]{1,0:T(4,128)S(1)} %get-tuple-element.85, pred[3072]{0:T(1024)(128)(4,1)S(1)} %lt.153), kind=kLoop, calls=%fused_computation.25 | loop fusion | flops 23591424 | bytes 18889728 | tf_op jit(solution)/shard_map/reduce_sum | solution.py:54
  153.0 12.2 %fusion.62 = bf16[384,4,88]{0,2,1:T(8,128)(2,1)} fusion(bf16[3072,4,88]{0,2,1:T(8,128)(2,1)} %reshape.480, f32[4,384,3072]{2,1,0:T(8,128)} %get-tuple-element.87, f32[4,384]{1,0:T(4,128)S(1)} %get-tuple-element.85, pred[3072]{0:T(1024)(128)(4,1)S(1)} %lt.153, f32[384,4]{0,1:T(4,128)S(1)} %bitcast_add_fusion.1, f32[384,4]{0,1:T(4,128)S(1)} %get-tuple-element.84), kind=kOutput, calls=%fused_computation.86 | convolution fusion | flops 854470656 | bytes 21328896 | tf_op jit(solution)/shard_map/chqk,ckhe->chqe/dot_general | solution.py:56
  170.3 7.5 all-to-all-start
  178.8 38.1 %all-reduce.2.cloned.1.call-done = bf16[384,1408]{1,0:T(8,128)(2,1)} async-done(((bf16[384,1408]{1,0:T(8,128)(2,1)}), bf16[384,1408]{1,0:T(8,128)(2,1)}) %all-reduce.2.cloned.1.call-update) | async-done | bytes 1081360 | tf_op jit(solution)/shard_map/psum | solution.py:133
  222.4 7.4 all-to-all-start.1
  229.8 3.7 fusion.57
  235.0 3.0 all-to-all-done.1
  238.1 4.0 scatter_custom_fusion
  242.1 3.0 fusion.23
  250.2 11.0 %stack.20 = bf16[32,2,4,512,128]{3,4,2,1,0:T(8,128)(2,1)} broadcast(bf16[2,4,512,128]{2,3,1,0:T(8,128)(2,1)S(1)} %copy.36), dimensions={1,2,3,4} | broadcast | bytes 34603008 | tf_op jit(solution)/shard_map/stack | solution.py:216
  261.2 8.4 all-to-all-start.2
  272.1 547.5 %all-to-all-done.2 = bf16[32,2,4,512,128]{3,4,2,1,0:T(8,128)(2,1)} async-done(((bf16[32,2,4,512,128]{3,4,2,1,0:T(8,128)(2,1)}), bf16[32,2,4,512,128]{3,4,2,1,0:T(8,128)(2,1)}, u32[]{:S(2)}, u32[]{:S(2)}) %all-to-all-start.2) | async-done | bytes 33554464 | tf_op jit(solution)/shard_map/all_to_all | solution.py:216
  819.5 217.1 %while.15 = (s32[]{:T(128)}, f32[4,2,512]{2,1,0:T(2,128)S(1)}, f32[4,2,512]{2,1,0:T(2,128)S(1)}, f32[4,2,512,64]{2,3,1,0:T(8,128)S(1)}, bf16[32,2,4,512,2,64]{3,...) while((s32[]{:T(128)}, f32[4,2,512]{2,1,0:T(2,128)S(1)}, ...), condition=%wide.region_19.20_spmd.clone, body=%wide.region_16.19_spmd.clone.sunk | while | flops 554455040 | bytes 29098120 | solution.py:232
  857.3 2.9 fusion.145
  931.9 2.9 fusion.145
  (288 shorter events, 255.2 us)
Async XLA Ops:
  6.5 212.6 %copy-start = (bf16[1408,512]{1,0:T(8,128)(2,1)S(1)}, bf16[1408,512]{1,0:T(8,128)(2,1)}, u32[]{:S(2)}) copy-start(bf16[1408,512]{1,0:T(8,128)(2,1)} %param.25) | copy-start | bytes 4325380
  6.5 3.3 copy-start.4
  6.5 3.3 copy-start.12
  6.5 3.3 copy-start.13
  6.5 210.3 %all-reduce.2.cloned.1.call-start = ((), (), s32[]{:S(2)}) async-start(), calls=%async_computation.3 | async-start | bytes 2162688 | tf_op jit(solution)/shard_map/psum | solution.py:133
  14.1 15.7 %collective-permute-start = (bf16[1,2,384,352]{2,3,1,0:T(8,128)(2,1)S(1)}, bf16[1,2,384,352]{2,3,1,0:T(8,128)(2,1)}, u32[]{:S(2)}, u32[]{:S(2)}) collective-permute-start(bf16[1,2,384,352]{2,3,1,0:T(8,128)(2,1)S(1)} %maximum_bitcast_fusion), channel_id=1, source_target_pairs={{0,16},{16,0},{4,20},{20,4},{8,24},{24,8},{12,28},{28,12},{32,48},... | collective-permute-start | bytes 1622024 | tf_op jit(solution)/shard_map/ppermute | solution.py:28
  32.2 25.1 %collective-permute-start.1 = (bf16[2,2,384,352]{2,3,1,0:T(8,128)(2,1)}, bf16[2,2,384,352]{2,3,1,0:T(8,128)(2,1)}, u32[]{:S(2)}, u32[]{:S(2)}) collective-permute-start(bf16[2,2,384,352]{2,3,1,0:T(8,128)(2,1)} %maximum_select_fusion.2), channel_id=1, source_target_pairs={{0,32},{32,0},{4,36},{36,4},{8,40},{40,8},{12,44},{44,12},{16,48},... | collective-permute-start | bytes 3244040 | tf_op jit(solution)/shard_map/ppermute | solution.py:28
  33.4 29.8 %copy-start.11 = (s32[4,96]{1,0:T(4,128)S(1)}, s32[4,96]{1,0:T(4,128)}, u32[]{:S(2)}) copy-start(s32[4,96]{1,0:T(4,128)} %param.18) | copy-start | bytes 4612
  61.2 48.9 %collective-permute-start.2 = (bf16[4,2,384,352]{2,3,1,0:T(8,128)(2,1)}, bf16[4,2,384,352]{2,3,1,0:T(8,128)(2,1)}, u32[]{:S(2)}, u32[]{:S(2)}) collective-permute-start(bf16[4,2,384,352]{2,3,1,0:T(8,128)(2,1)} %maximum_select_fusion.1), channel_id=1, source_target_pairs={{0,64},{64,0},{4,68},{68,4},{8,72},{72,8},{12,76},{76,12},{16,80},... | collective-permute-start | bytes 6488072 | tf_op jit(solution)/shard_map/ppermute | solution.py:28
  153.0 12.2 %copy-start.6 = (bf16[352,1408]{1,0:T(8,128)(2,1)S(1)}, bf16[352,1408]{1,0:T(8,128)(2,1)}, u32[]{:S(2)}) copy-start(bf16[352,1408]{1,0:T(8,128)(2,1)} %param.22) | copy-start | bytes 2973700
  170.3 52.1 %all-to-all-start = ((s32[32,1,12]{2,1,0:T(1,128)}), s32[32,1,12]{2,1,0:T(1,128)S(1)}, u32[]{:S(2)}, u32[]{:S(2)}) async-start(s32[32,1,12]{2,1,0:T(1,128)} %bitcast.3), calls=%async_computation | async-start | bytes 32768 | tf_op jit(solution)/shard_map/all_to_all | solution.py:172
  178.7 40.4 %copy-start.14 = (f32[1408]{0:T(1024)S(1)}, f32[1408]{0:T(1024)}, u32[]{:S(2)}) copy-start(f32[1408]{0:T(1024)} %param.24) | copy-start | bytes 16900
  178.7 40.4 %copy-start.15 = (f32[1408]{0:T(1024)S(1)}, f32[1408]{0:T(1024)}, u32[]{:S(2)}) copy-start(f32[1408]{0:T(1024)} %param.23) | copy-start | bytes 16900
  216.9 1.7 copy-start.5
  222.4 15.6 %all-to-all-start.1 = ((bf16[32,12,512]{2,1,0:T(8,128)(2,1)}), bf16[32,12,512]{2,1,0:T(8,128)(2,1)S(1)}, u32[]{:S(2)}, u32[]{:S(2)}) async-start(bf16[32,12,512]{2,1,0:T(8,128)(2,1)} %reshape.481), calls=%async_computation.1 | async-start | bytes 1048576 | tf_op jit(solution)/shard_map/all_to_all | solution.py:171
  238.1 4.0 copy-start.8
  242.1 3.4 copy-start.2
  245.5 1.3 copy-start.9
  245.5 1.3 copy-start.10
  246.9 1.2 copy-start.7
  248.1 1.4 copy-start.3
  261.2 558.3 %all-to-all-start.2 = ((bf16[32,2,4,512,128]{3,4,2,1,0:T(8,128)(2,1)}), bf16[32,2,4,512,128]{3,4,2,1,0:T(8,128)(2,1)}, u32[]{:S(2)}, u32[]{:S(2)}) async-start(bf16[32,2,4,512,128]{3,4,2,1,0:T(8,128)(2,1)} %stack.20), calls=%async_computation.2 | async-start | bytes 67108864 | tf_op jit(solution)/shard_map/all_to_all | solution.py:216
  1036.6 2.2 copy-start.1
Sparse Core Ops, SparseCore 0:
  168.1 48.7 all-reduce.1
